TPU v7x, 32 devices: a whole 2x2x4 slice. The times are simulated.
32 devices in a mesh: replica: 8 (over y, x, core), group: 4 (over z).
Axes of the slice: x: 2, y: 2, z: 4, core: 2. Of those that a mesh axis runs over, the one named last changes fastest.
Arguments:
- inputs: bfloat16 [8, 512, 2048], P('replica', 'group'), may hold values from -6 to 6
- seq_lengths: int32 [8], P('replica'), may hold values from 128 to 512, as said below
- bucket_ids: int32 [1023], replicated, may hold values from 0 to 31, as said below
- norm1_gain: bfloat16 [2048], P('group'), may hold values from 0.25 to 1.75
- w_query: bfloat16 [2048, 2048], P(None, 'group'), may hold values from -0.0625 to 0.0625
- w_key: bfloat16 [2048, 2048], P(None, 'group'), may hold values from -0.0625 to 0.0625
- w_value: bfloat16 [2048, 2048], P(None, 'group'), may hold values from -0.125 to 0.125
- w_attn_out: bfloat16 [2048, 2048], P('group'), may hold values from -0.5 to 0.5
- bias_table: bfloat16 [32, 32], P(None, 'group'), may hold values from -4 to 4
- norm2_gain: bfloat16 [2048], P('group'), may hold values from 0.25 to 1.75
- w_gate: bfloat16 [2048, 5120], P(None, 'group'), may hold values from -0.125 to 0.125
- w_up: bfloat16 [2048, 5120], P(None, 'group'), may hold values from -0.125 to 0.125
- w_ffn_out: bfloat16 [5120, 2048], P('group'), may hold values from -0.078125 to 0.078125
- cotangent: bfloat16 [8, 512, 2048], P('replica', 'group'), may hold values from -6 to 6
Outputs:
- result: bfloat16 [8, 512, 2048], P('replica', 'group')
- input_grad: bfloat16 [8, 512, 2048], P('replica', 'group')
- norm1_gain_grad: float32 [2048], P('group')
- query_grad: float32 [2048, 2048], P(None, 'group')
- key_grad: float32 [2048, 2048], P(None, 'group')
- value_grad: float32 [2048, 2048], P(None, 'group')
- attn_out_grad: float32 [2048, 2048], P('group')
- bias_table_grad: float32 [32, 32], P(None, 'group')
- norm2_gain_grad: float32 [2048], P('group')
- gate_grad: float32 [2048, 5120], P(None, 'group')
- up_grad: float32 [2048, 5120], P(None, 'group')
- ffn_out_grad: float32 [5120, 2048], P('group')
Inputs may be any that keep to these rules, and one draw needn't show every extreme that they name: `seq_lengths`: one sequence has exactly 512 valid positions and another exactly 128. `bucket_ids`: entry 511 + o is the bucket of the offset o = key position - query position; every bucket occurs.
All inputs are finite; a program needn't handle non-finite values.
Results may differ from a plain program's by a relative error of at most 0.02.
Values may be sent and summed in bfloat16 or wider, within the bound.
A program may use at most 448 MiB of HBM per device.

v0:
```python
import jax
import jax.numpy as jnp
from jax import lax
from jax.sharding import PartitionSpec as P

epsilon = 1e-06
negative = -1000000000.0
head_block = 8
highest = lax.Precision.HIGHEST


def rms_scale(values, gain):
    return values * lax.rsqrt(jnp.mean(values * values, axis=-1, keepdims=True) + epsilon) * gain


def gated_gelu(gate_pre, up_pre):
    return jax.nn.gelu(gate_pre, approximate=True) * up_pre


def inner_rows(left, right):
    return lax.dot_general(
        left, right, (((0,), (0,)), ((), ())), preferred_element_type=jnp.float32
    )


def inner_columns(left, right):
    return lax.dot_general(
        left, right, (((1,), (1,)), ((), ())), preferred_element_type=jnp.float32
    )


def split_heads(matrix, groups, block_size):
    return matrix.reshape(matrix.shape[0], groups, block_size, -1).transpose(1, 0, 2, 3)


def merge_heads(blocks):
    return blocks.transpose(1, 0, 2, 3).reshape(blocks.shape[1], -1)


def spread_offsets(vector, row_count, col_count):
    span_width = row_count + col_count + 1
    block_heads = vector.shape[0]
    tiled_rows = jnp.broadcast_to(vector[:, None, :], (block_heads, row_count, span_width))
    flattened = tiled_rows.reshape(block_heads, row_count * span_width)[
        :, : row_count * (span_width - 1)
    ]
    return flattened.reshape(block_heads, row_count, span_width - 1)[:, :, row_count:]


def fold_offsets(matrix):
    block_heads, row_count, col_count = matrix.shape
    padded = jnp.pad(matrix, ((0, 0), (0, 0), (row_count, 0)))
    flattened = jnp.pad(
        padded.reshape(block_heads, row_count * (row_count + col_count)), ((0, 0), (0, row_count))
    )
    sums_all = flattened.reshape(block_heads, row_count, row_count + col_count + 1).sum(axis=1)
    return sums_all[:, 1 : row_count + col_count]


def offset_table(table_part, one_hot, groups, block_size):
    per_offset = jnp.dot(one_hot, table_part.astype(jnp.float32), precision=highest)
    return jnp.pad(per_offset.T, ((0, 0), (1, 1))).reshape(groups, block_size, -1)


def attention_forward(query_low, key_all, value_all, offsets, key_valid, groups, block_size):
    row_count = query_low.shape[0]
    keys_total = key_all.shape[0]

    def attend_block(operands):
        query_blk, key_blk, value_blk, offset_blk = operands
        scores = jnp.einsum("qhd,khd->hqk", query_blk, key_blk, preferred_element_type=jnp.float32)
        scores = jnp.where(
            key_valid, scores + spread_offsets(offset_blk, row_count, keys_total), negative
        )
        top_score = jnp.max(scores, axis=-1, keepdims=True)
        weights_exp = jnp.exp(scores - top_score)
        total_exp = jnp.sum(weights_exp, axis=-1, keepdims=True)
        probs_low = (weights_exp / total_exp).astype(jnp.bfloat16)
        attended_blk = jnp.einsum(
            "hqk,khd->qhd", probs_low, value_blk, preferred_element_type=jnp.float32
        )
        return (attended_blk, top_score[..., 0] + jnp.log(total_exp[..., 0]))

    operands = (
        split_heads(query_low, groups, block_size),
        split_heads(key_all, groups, block_size),
        split_heads(value_all, groups, block_size),
        offsets,
    )
    attended, log_totals = lax.map(attend_block, operands)
    return (merge_heads(attended).astype(jnp.bfloat16), log_totals)


def attention_backward(
    query_low, key_all, value_all, offsets, key_valid, grad_attended, log_totals, groups, block_size
):
    row_count = query_low.shape[0]
    keys_total = key_all.shape[0]

    def attend_back(operands):
        query_blk, key_blk, value_blk, offset_blk, grad_blk, log_blk = operands
        scores = jnp.einsum("qhd,khd->hqk", query_blk, key_blk, preferred_element_type=jnp.float32)
        scores = jnp.where(
            key_valid, scores + spread_offsets(offset_blk, row_count, keys_total), negative
        )
        probs = jnp.exp(scores - log_blk[..., None])
        grad_probs = jnp.einsum(
            "qhd,khd->hqk", grad_blk, value_blk, preferred_element_type=jnp.float32
        )
        inner_sum = jnp.sum(probs * grad_probs, axis=-1, keepdims=True)
        grad_scores = (probs * (grad_probs - inner_sum)).astype(jnp.bfloat16)
        probs_low = probs.astype(jnp.bfloat16)
        grad_query = jnp.einsum(
            "hqk,khd->qhd", grad_scores, key_blk, preferred_element_type=jnp.float32
        )
        grad_key = jnp.einsum(
            "hqk,qhd->khd", grad_scores, query_blk, preferred_element_type=jnp.float32
        )
        grad_value = jnp.einsum(
            "hqk,qhd->khd", probs_low, grad_blk, preferred_element_type=jnp.float32
        )
        return (grad_query, grad_key, grad_value, fold_offsets(grad_scores.astype(jnp.float32)))

    operands = (
        split_heads(query_low, groups, block_size),
        split_heads(key_all, groups, block_size),
        split_heads(value_all, groups, block_size),
        offsets,
        split_heads(grad_attended, groups, block_size),
        log_totals,
    )
    grad_query_blk, grad_key_blk, grad_value_blk, offset_sums = lax.map(attend_back, operands)
    return (
        merge_heads(grad_query_blk),
        merge_heads(grad_key_blk),
        merge_heads(grad_value_blk),
        offset_sums,
    )


def local(
    inputs,
    seq_lengths,
    bucket_ids,
    norm1_gain,
    w_query,
    w_key,
    w_value,
    w_attn_out,
    bias_table,
    norm2_gain,
    w_gate,
    w_up,
    w_ffn_out,
    cotangent,
):
    hidden_in = inputs[0].astype(jnp.float32)
    row_count = hidden_in.shape[0]
    keys_total = row_count * lax.axis_size("group")
    query_start = lax.axis_index("group") * row_count
    length = seq_lengths[0]
    buckets = bias_table.shape[0]
    key_valid = (jnp.arange(keys_total) < length)[None, None, :]
    row_valid = query_start + jnp.arange(row_count) < length
    gain_one, gain_two, query_full, key_full, value_full, attn_full, table_full = (
        lax.all_gather(norm1_gain, "group", axis=0, tiled=True),
        lax.all_gather(norm2_gain, "group", axis=0, tiled=True),
        lax.all_gather(w_query, "group", axis=1, tiled=True),
        lax.all_gather(w_key, "group", axis=1, tiled=True),
        lax.all_gather(w_value, "group", axis=1, tiled=True),
        lax.all_gather(w_attn_out, "group", axis=0, tiled=True),
        lax.all_gather(bias_table, "group", axis=1, tiled=True),
    )
    gain_first = gain_one.astype(jnp.float32)
    gain_second = gain_two.astype(jnp.float32)
    head_count = table_full.shape[1]
    groups = head_count // head_block
    normed_one = rms_scale(hidden_in, gain_first).astype(jnp.bfloat16)
    query_low = jnp.dot(normed_one, query_full, preferred_element_type=jnp.float32).astype(
        jnp.bfloat16
    )
    key_low = jnp.dot(normed_one, key_full, preferred_element_type=jnp.float32).astype(jnp.bfloat16)
    value_low = jnp.dot(normed_one, value_full, preferred_element_type=jnp.float32).astype(
        jnp.bfloat16
    )
    key_all, value_all = (
        lax.all_gather(key_low, "group", axis=0, tiled=True),
        lax.all_gather(value_low, "group", axis=0, tiled=True),
    )
    window = lax.dynamic_slice_in_dim(
        bucket_ids, keys_total - row_count - query_start, row_count + keys_total - 1
    )
    one_hot = (window[:, None] == jnp.arange(buckets)[None, :]).astype(jnp.float32)
    offsets = offset_table(table_full, one_hot, groups, head_block)
    attended_low, log_totals = attention_forward(
        query_low, key_all, value_all, offsets, key_valid, groups, head_block
    )
    middle = hidden_in + jnp.dot(attended_low, attn_full, preferred_element_type=jnp.float32)
    normed_two = rms_scale(middle, gain_second).astype(jnp.bfloat16)
    grad_out = cotangent[0].astype(jnp.float32) * row_valid[:, None].astype(jnp.float32)
    grad_low = grad_out.astype(jnp.bfloat16)
    gate_full, up_full, ffn_full = (
        lax.all_gather(w_gate, "group", axis=1, tiled=True),
        lax.all_gather(w_up, "group", axis=1, tiled=True),
        lax.all_gather(w_ffn_out, "group", axis=0, tiled=True),
    )
    gate_pre = jnp.dot(normed_two, gate_full, preferred_element_type=jnp.float32)
    up_pre = jnp.dot(normed_two, up_full, preferred_element_type=jnp.float32)
    hidden_low = gated_gelu(gate_pre, up_pre).astype(jnp.bfloat16)
    branch_ffn = jnp.dot(hidden_low, ffn_full, preferred_element_type=jnp.float32)
    result = (middle + branch_ffn).astype(jnp.bfloat16)
    gate_back, up_back, ffn_back = (
        lax.all_gather(w_gate, "group", axis=1, tiled=True),
        lax.all_gather(w_up, "group", axis=1, tiled=True),
        lax.all_gather(w_ffn_out, "group", axis=0, tiled=True),
    )
    grad_hidden = inner_columns(grad_low, ffn_back)
    _, pull_gelu = jax.vjp(gated_gelu, gate_pre, up_pre)
    grad_gate, grad_up = pull_gelu(grad_hidden)
    grad_gate = grad_gate.astype(jnp.bfloat16)
    grad_up = grad_up.astype(jnp.bfloat16)
    grad_normed = inner_columns(grad_gate, gate_back) + inner_columns(grad_up, up_back)
    gate_grad, up_grad, ffn_out_grad = (
        lax.psum_scatter(
            inner_rows(normed_two, grad_gate).astype(jnp.bfloat16),
            "group",
            scatter_dimension=1,
            tiled=True,
        ).astype(jnp.float32),
        lax.psum_scatter(
            inner_rows(normed_two, grad_up).astype(jnp.bfloat16),
            "group",
            scatter_dimension=1,
            tiled=True,
        ).astype(jnp.float32),
        lax.psum_scatter(
            inner_rows(hidden_low, grad_low).astype(jnp.bfloat16),
            "group",
            scatter_dimension=0,
            tiled=True,
        ).astype(jnp.float32),
    )
    _, pull_two = jax.vjp(rms_scale, middle, gain_second)
    grad_mid_norm, gain_two_grad = pull_two(grad_normed)
    grad_middle = grad_out + grad_mid_norm
    grad_branch = grad_middle.astype(jnp.bfloat16)
    query_back, key_back, value_back, attn_back, table_back = (
        lax.all_gather(w_query, "group", axis=1, tiled=True),
        lax.all_gather(w_key, "group", axis=1, tiled=True),
        lax.all_gather(w_value, "group", axis=1, tiled=True),
        lax.all_gather(w_attn_out, "group", axis=0, tiled=True),
        lax.all_gather(bias_table, "group", axis=1, tiled=True),
    )
    attn_out_grad = inner_rows(attended_low, grad_branch)
    grad_attended = inner_columns(grad_branch, attn_back).astype(jnp.bfloat16)
    offset_bwd = offset_table(table_back, one_hot, groups, head_block)
    grad_query, grad_key, grad_value, offset_sums = attention_backward(
        query_low,
        key_all,
        value_all,
        offset_bwd,
        key_valid,
        grad_attended,
        log_totals,
        groups,
        head_block,
    )
    key_sum, value_sum = (
        lax.psum_scatter(
            grad_key.astype(jnp.bfloat16), "group", scatter_dimension=0, tiled=True
        ).astype(jnp.float32),
        lax.psum_scatter(
            grad_value.astype(jnp.bfloat16), "group", scatter_dimension=0, tiled=True
        ).astype(jnp.float32),
    )
    grad_query_low = grad_query.astype(jnp.bfloat16)
    grad_key_low = key_sum.astype(jnp.bfloat16)
    grad_value_low = value_sum.astype(jnp.bfloat16)
    table_grad = jnp.dot(offset_sums.reshape(head_count, -1), one_hot, precision=highest).T
    query_grad = inner_rows(normed_one, grad_query_low)
    key_grad = inner_rows(normed_one, grad_key_low)
    value_grad = inner_rows(normed_one, grad_value_low)
    grad_normed_one = (
        inner_columns(grad_query_low, query_back)
        + inner_columns(grad_key_low, key_back)
        + inner_columns(grad_value_low, value_back)
    )
    _, pull_one = jax.vjp(rms_scale, hidden_in, gain_first)
    grad_in_norm, gain_one_grad = pull_one(grad_normed_one)
    input_grad = (grad_middle + grad_in_norm).astype(jnp.bfloat16)
    gain_one_part, gain_two_part, query_part, key_part, value_part, attn_part, table_part = (
        lax.psum_scatter(
            gain_one_grad.astype(jnp.bfloat16), "group", scatter_dimension=0, tiled=True
        ).astype(jnp.float32),
        lax.psum_scatter(
            gain_two_grad.astype(jnp.bfloat16), "group", scatter_dimension=0, tiled=True
        ).astype(jnp.float32),
        lax.psum_scatter(
            query_grad.astype(jnp.bfloat16), "group", scatter_dimension=1, tiled=True
        ).astype(jnp.float32),
        lax.psum_scatter(
            key_grad.astype(jnp.bfloat16), "group", scatter_dimension=1, tiled=True
        ).astype(jnp.float32),
        lax.psum_scatter(
            value_grad.astype(jnp.bfloat16), "group", scatter_dimension=1, tiled=True
        ).astype(jnp.float32),
        lax.psum_scatter(
            attn_out_grad.astype(jnp.bfloat16), "group", scatter_dimension=0, tiled=True
        ).astype(jnp.float32),
        lax.psum_scatter(
            table_grad.astype(jnp.bfloat16), "group", scatter_dimension=1, tiled=True
        ).astype(jnp.float32),
    )
    summed = (
        lax.psum(gain_one_part.astype(jnp.bfloat16), "replica").astype(jnp.float32),
        lax.psum(query_part.astype(jnp.bfloat16), "replica").astype(jnp.float32),
        lax.psum(key_part.astype(jnp.bfloat16), "replica").astype(jnp.float32),
        lax.psum(value_part.astype(jnp.bfloat16), "replica").astype(jnp.float32),
        lax.psum(attn_part.astype(jnp.bfloat16), "replica").astype(jnp.float32),
        lax.psum(table_part.astype(jnp.bfloat16), "replica").astype(jnp.float32),
        lax.psum(gain_two_part.astype(jnp.bfloat16), "replica").astype(jnp.float32),
        lax.psum(gate_grad.astype(jnp.bfloat16), "replica").astype(jnp.float32),
        lax.psum(up_grad.astype(jnp.bfloat16), "replica").astype(jnp.float32),
        lax.psum(ffn_out_grad.astype(jnp.bfloat16), "replica").astype(jnp.float32),
    )
    return (
        result[None],
        input_grad[None],
        summed[0],
        summed[1],
        summed[2],
        summed[3],
        summed[4],
        summed[5],
        summed[6],
        summed[7],
        summed[8],
        summed[9],
    )


def solution(mesh):
    placed = (
        P("replica", "group", None),
        P("replica"),
        P(),
        P("group"),
        P(None, "group"),
        P(None, "group"),
        P(None, "group"),
        P("group", None),
        P(None, "group"),
        P("group"),
        P(None, "group"),
        P(None, "group"),
        P("group", None),
        P("replica", "group", None),
    )
    return jax.shard_map(
        local,
        mesh=mesh,
        in_specs=placed,
        out_specs=(
            P("replica", "group", None),
            P("replica", "group", None),
            P("group"),
            P(None, "group"),
            P(None, "group"),
            P(None, "group"),
            P("group", None),
            P(None, "group"),
            P("group"),
            P(None, "group"),
            P(None, "group"),
            P("group", None),
        ),
        check_vma=False,
    )
```

profile of v0, /device:TPU:0, one launch (start us, length us, event | category | flops | bytes accessed | tf_op | source)
XLA Modules:
  0.0 4007.4 jit_solution(15519130537218076561)
XLA Ops:
  9.5 13.5 all-gather
  23.3 138.7 %all-gather.12.cloned.1.call-done = bf16[2048,2048]{1,0:T(8,128)(2,1)} async-done(((bf16[2048,512]{1,0:T(8,128)(2,1)}), bf16[2048,2048]{1,0:T(8,128)(2,1)}) %all-gather.12.cloned.1.call-update) | async-done | bytes 8388624 | tf_op jit(solution)/shard_map/all_gather | solution.py:170
  167.5 143.9 %all-gather.18.cloned.1.call-done = bf16[2048,2048]{1,0:T(8,128)(2,1)} async-done(((bf16[2048,512]{1,0:T(8,128)(2,1)}), bf16[2048,2048]{1,0:T(8,128)(2,1)}) %all-gather.18.cloned.1.call-update) | async-done | bytes 8388624 | tf_op jit(solution)/shard_map/all_gather | solution.py:169
  319.9 15.4 all-gather.1
  336.0 13.7 all_gather.50
  350.1 110.9 %all-gather.16.cloned.1.call-done = bf16[2048,2048]{1,0:T(8,128)(2,1)} async-done(((bf16[2048,512]{1,0:T(8,128)(2,1)}), bf16[2048,2048]{1,0:T(8,128)(2,1)}) %all-gather.16.cloned.1.call-update) | async-done | bytes 8388624 | tf_op jit(solution)/shard_map/all_gather | solution.py:168
  466.8 40.4 %all-gather.14.cloned.1.call-done = bf16[512,2048]{1,0:T(8,128)(2,1)} async-done(((bf16[128,2048]{1,0:T(8,128)(2,1)}), bf16[512,2048]{1,0:T(8,128)(2,1)}) %all-gather.14.cloned.1.call-update) | async-done | bytes 2097168 | tf_op jit(solution)/shard_map/all_gather | solution.py:188
  511.1 42.8 %all-gather.20.cloned.1.call-done = bf16[512,2048]{1,0:T(8,128)(2,1)} async-done(((bf16[128,2048]{1,0:T(8,128)(2,1)}), bf16[512,2048]{1,0:T(8,128)(2,1)}) %all-gather.20.cloned.1.call-update) | async-done | bytes 2097168 | tf_op jit(solution)/shard_map/all_gather | solution.py:187
  558.7 46.0 %while.32 = (s32[]{:T(128)}, bf16[4,128,8,64]{1,3,2,0:T(8,128)(2,1)}, f32[4,8,128]{2,1,0:T(8,128)S(1)}, bf16[4,512,8,64]{1,3,2,0:T(8,128)(2,1)}, bf16[4,128,8,64...) while((s32[]{:T(128)}, ...), condition=%wide.region_4.5_spmd.clone, body=%wide.region_1.4_spmd.clone.sunk | while | flops 138411520 | bytes 35106080 | solution.py:90
  604.7 98.9 %all-gather.22.cloned.1.call-done = bf16[2048,2048]{1,0:T(8,128)(2,1)} async-done(((bf16[512,2048]{1,0:T(8,128)(2,1)}), bf16[2048,2048]{1,0:T(8,128)(2,1)}) %all-gather.22.cloned.1.call-update) | async-done | bytes 8388624 | tf_op jit(solution)/shard_map/all_gather | solution.py:171
  708.8 351.5 %all-gather.24.cloned.1.call-done = bf16[2048,5120]{1,0:T(8,128)(2,1)} async-done(((bf16[2048,1280]{1,0:T(8,128)(2,1)}), bf16[2048,5120]{1,0:T(8,128)(2,1)}) %all-gather.24.cloned.1.call-update) | async-done | bytes 20971536 | tf_op jit(solution)/shard_map/all_gather | solution.py:203
  1060.3 11.7 fusion.89
  1072.1 345.3 %all-gather.26.cloned.1.call-done = bf16[2048,5120]{1,0:T(8,128)(2,1)} async-done(((bf16[2048,1280]{1,0:T(8,128)(2,1)}), bf16[2048,5120]{1,0:T(8,128)(2,1)}) %all-gather.26.cloned.1.call-update) | async-done | bytes 20971536 | tf_op jit(solution)/shard_map/all_gather | solution.py:204
  1417.4 11.7 fusion.90
  1429.1 345.3 %all-gather.28.cloned.1.call-done = bf16[5120,2048]{1,0:T(8,128)(2,1)} async-done(((bf16[1280,2048]{1,0:T(8,128)(2,1)}), bf16[5120,2048]{1,0:T(8,128)(2,1)}) %all-gather.28.cloned.1.call-update) | async-done | bytes 20971536 | tf_op jit(solution)/shard_map/all_gather | solution.py:205
  1774.4 14.3 multiply_convert_fusion.1
  1788.7 12.4 fusion.91
  1801.1 13.4 multiply_reduce_fusion.1
  1822.0 106.5 %while.33 = (s32[]{:T(128)}, bf16[4,128,8,64]{1,3,2,0:T(8,128)(2,1)}, bf16[4,512,8,64]{1,3,2,0:T(8,128)(2,1)}, bf16[4,512,8,64]{1,3,2,0:T(8,128)(2,1)}, f32[4,8,...) while((s32[]{:T(128)}, ...), condition=%wide.region_10.11_spmd.clone, body=%wide.region_7.10_spmd.clone.sunk | while | flops 341570048 | bytes 102152648 | solution.py:132
  1949.1 26.1 reduce-scatter.28.cloned.1.call-done
  1982.1 39.2 reduce-scatter.30.cloned.1.call-done
  2063.4 104.6 %reduce-scatter.14.cloned.1.call-done = bf16[2048,512]{1,0:T(8,128)(2,1)} async-done(((bf16[2048,2048]{1,0:T(8,128)(2,1)}), bf16[2048,512]{1,0:T(8,128)(2,1)}) %reduce-scatter.14.cloned.1.call-update) | async-done | bytes 2097168 | tf_op jit(solution)/shard_map/reduce_scatter | solution.py:298
  2168.0 147.6 %reduce-scatter.20.cloned.1.call-done = bf16[512,2048]{1,0:T(8,128)(2,1)} async-done(((bf16[2048,2048]{1,0:T(8,128)(2,1)}), bf16[512,2048]{1,0:T(8,128)(2,1)}) %reduce-scatter.20.cloned.1.call-update) | async-done | bytes 2097168 | tf_op jit(solution)/shard_map/reduce_scatter | solution.py:307
  2315.6 148.0 %reduce-scatter.16.cloned.1.call-done = bf16[2048,512]{1,0:T(8,128)(2,1)} async-done(((bf16[2048,2048]{1,0:T(8,128)(2,1)}), bf16[2048,512]{1,0:T(8,128)(2,1)}) %reduce-scatter.16.cloned.1.call-update) | async-done | bytes 2097168 | tf_op jit(solution)/shard_map/reduce_scatter | solution.py:301
  2463.6 148.0 %reduce-scatter.18.cloned.1.call-done = bf16[2048,512]{1,0:T(8,128)(2,1)} async-done(((bf16[2048,2048]{1,0:T(8,128)(2,1)}), bf16[2048,512]{1,0:T(8,128)(2,1)}) %reduce-scatter.18.cloned.1.call-update) | async-done | bytes 2097168 | tf_op jit(solution)/shard_map/reduce_scatter | solution.py:304
  2611.6 350.2 %reduce-scatter.22.cloned.1.call-done = bf16[2048,1280]{1,0:T(8,128)(2,1)} async-done(((bf16[2048,5120]{1,0:T(8,128)(2,1)}), bf16[2048,1280]{1,0:T(8,128)(2,1)}) %reduce-scatter.22.cloned.1.call-update) | async-done | bytes 5242896 | tf_op jit(solution)/shard_map/reduce_scatter | solution.py:224
  2961.8 351.0 %reduce-scatter.24.cloned.1.call-done = bf16[2048,1280]{1,0:T(8,128)(2,1)} async-done(((bf16[2048,5120]{1,0:T(8,128)(2,1)}), bf16[2048,1280]{1,0:T(8,128)(2,1)}) %reduce-scatter.24.cloned.1.call-update) | async-done | bytes 5242896 | tf_op jit(solution)/shard_map/reduce_scatter | solution.py:230
  3312.8 350.9 %reduce-scatter.26.cloned.1.call-done = bf16[1280,2048]{1,0:T(8,128)(2,1)} async-done(((bf16[5120,2048]{1,0:T(8,128)(2,1)}), bf16[1280,2048]{1,0:T(8,128)(2,1)}) %reduce-scatter.26.cloned.1.call-update) | async-done | bytes 5242896 | tf_op jit(solution)/shard_map/reduce_scatter | solution.py:236
  3673.3 11.9 fusion.51
  3691.3 18.9 all-reduce.8
  3710.3 13.0 all-reduce.6
  3726.2 245.3 %all-reduce.11.cloned.1.call-done = (bf16[2048,512]{1,0:T(8,128)(2,1)}, bf16[2048,512]{1,0:T(8,128)(2,1)}, bf16[2048,512]{1,0:T(8,128)(2,1)}, bf16[512,2048]{1,0...) async-done(((bf16[2048,512]{1,0:T(8,128)(2,1)}, bf16[2048,512]{1,0:T(8,128)(2,1)}, bf16[2048,512]{1,0:T(8,128)(2,1)}, ...) | async-done | bytes 24117264 | tf_op jit(solution)/shard_map/psum | solution.py:316
  (376 shorter events, 310.5 us)
Async XLA Ops:
  7.2 154.8 %all-gather.12.cloned.1.call-start = ((), (), s32[]{:S(2)}) async-start(), calls=%async_computation.9 | async-start | bytes 10485760 | tf_op jit(solution)/shard_map/all_gather | solution.py:170
  7.9 303.5 %all-gather.18.cloned.1.call-start = ((), (), s32[]{:S(2)}) async-start(), calls=%async_computation.12 | async-start | bytes 10485760 | tf_op jit(solution)/shard_map/all_gather | solution.py:169
  8.7 452.4 %all-gather.16.cloned.1.call-start = ((), (), s32[]{:S(2)}) async-start(), calls=%async_computation.11 | async-start | bytes 10485760 | tf_op jit(solution)/shard_map/all_gather | solution.py:168
  9.4 497.8 %all-gather.14.cloned.1.call-start = ((), (), s32[]{:S(2)}) async-start(), calls=%async_computation.10 | async-start | bytes 2621440 | tf_op jit(solution)/shard_map/all_gather | solution.py:188
  23.1 438.0 %copy-start.16 = (f32[4,1,512]{2,1,0:T(1,128)}, f32[4,1,512]{2,1,0:T(1,128)S(1)}, u32[]{:S(2)}) copy-start(f32[4,1,512]{2,1,0:T(1,128)S(1)} %convert_element_type.283) | copy-start | bytes 24580
  23.3 144.2 %copy-start.39 = (f32[128]{0:T(128)}, f32[128]{0:T(128)S(1)}, u32[]{:S(2)}) copy-start(f32[128]{0:T(128)S(1)} %fusion.60) | copy-start | bytes 1540
  23.3 437.8 %copy-start.30 = (f32[128]{0:T(128)}, f32[128]{0:T(128)S(1)}, u32[]{:S(2)}) copy-start(f32[128]{0:T(128)S(1)} %fusion.81) | copy-start | bytes 1540
  167.5 386.4 %all-gather.20.cloned.1.call-start = ((), (), s32[]{:S(2)}) async-start(), calls=%async_computation.13 | async-start | bytes 2621440 | tf_op jit(solution)/shard_map/all_gather | solution.py:187
  316.9 386.8 %all-gather.22.cloned.1.call-start = ((), (), s32[]{:S(2)}) async-start(), calls=%async_computation.14 | async-start | bytes 10485760 | tf_op jit(solution)/shard_map/all_gather | solution.py:171
  317.5 742.9 %all-gather.24.cloned.1.call-start = ((), (), s32[]{:S(2)}) async-start(), calls=%async_computation.15 | async-start | bytes 26214400 | tf_op jit(solution)/shard_map/all_gather | solution.py:203
  318.2 1099.1 %all-gather.26.cloned.1.call-start = ((), (), s32[]{:S(2)}) async-start(), calls=%async_computation.16 | async-start | bytes 26214400 | tf_op jit(solution)/shard_map/all_gather | solution.py:204
  319.0 17.0 copy-start.33
  319.0 17.0 copy-start.36
  319.0 1455.4 %all-gather.28.cloned.1.call-start = ((), (), s32[]{:S(2)}) async-start(), calls=%async_computation.17 | async-start | bytes 26214400 | tf_op jit(solution)/shard_map/all_gather | solution.py:205
  319.7 1655.4 %reduce-scatter.28.cloned.1.call-start = ((), (), s32[]{:S(2)}) async-start(), calls=%async_computation.25 | async-start | bytes 2621440
  336.0 129.7 %copy-start.34 = (s32[639]{0:T(1024)}, s32[639]{0:T(1024)S(1)}, u32[]{:S(2)}) copy-start(s32[639]{0:T(1024)S(1)} %dynamic_slice.55) | copy-start | bytes 7672
  708.6 1105.9 %copy-start.3 = (f32[128,2048]{1,0:T(8,128)}, f32[128,2048]{1,0:T(8,128)S(1)}, u32[]{:S(2)}) copy-start(f32[128,2048]{1,0:T(8,128)S(1)} %get-tuple-element.324) | copy-start | bytes 3145732
  708.8 708.6 %copy-start.7 = (bf16[128,2048]{1,0:T(8,128)(2,1)}, bf16[128,2048]{1,0:T(8,128)(2,1)S(1)}, u32[]{:S(2)}) copy-start(bf16[128,2048]{1,0:T(8,128)(2,1)S(1)} %multiply_convert_fusion.3) | copy-start | bytes 1572868
  1072.1 702.3 %copy-start.18 = (bf16[1,128,2048]{2,1,0:T(8,128)(2,1)S(1)}, bf16[1,128,2048]{2,1,0:T(8,128)(2,1)}, u32[]{:S(2)}) copy-start(bf16[1,128,2048]{2,1,0:T(8,128)(2,1)} %param.31) | copy-start | bytes 1572868
  1801.1 16.1 slice-start.3
  1932.6 88.8 %reduce-scatter.30.cloned.1.call-start = ((), (), s32[]{:S(2)}) async-start(), calls=%async_computation.26 | async-start | bytes 2621440
  1935.1 232.9 %reduce-scatter.14.cloned.1.call-start = ((), (), s32[]{:S(2)}) async-start(), calls=%async_computation.18 | async-start | bytes 10485760 | tf_op jit(solution)/shard_map/reduce_scatter | solution.py:298
  1942.1 373.5 %reduce-scatter.20.cloned.1.call-start = ((), (), s32[]{:S(2)}) async-start(), calls=%async_computation.21 | async-start | bytes 10485760 | tf_op jit(solution)/shard_map/reduce_scatter | solution.py:307
  1949.0 514.6 %reduce-scatter.16.cloned.1.call-start = ((), (), s32[]{:S(2)}) async-start(), calls=%async_computation.19 | async-start | bytes 10485760 | tf_op jit(solution)/shard_map/reduce_scatter | solution.py:301
  1982.1 629.5 %reduce-scatter.18.cloned.1.call-start = ((), (), s32[]{:S(2)}) async-start(), calls=%async_computation.20 | async-start | bytes 10485760 | tf_op jit(solution)/shard_map/reduce_scatter | solution.py:304
  2028.3 933.5 %reduce-scatter.22.cloned.1.call-start = ((), (), s32[]{:S(2)}) async-start(), calls=%async_computation.22 | async-start | bytes 26214400 | tf_op jit(solution)/shard_map/reduce_scatter | solution.py:224
  2040.2 1272.6 %reduce-scatter.24.cloned.1.call-start = ((), (), s32[]{:S(2)}) async-start(), calls=%async_computation.23 | async-start | bytes 26214400 | tf_op jit(solution)/shard_map/reduce_scatter | solution.py:230
  2051.7 1612.0 %reduce-scatter.26.cloned.1.call-start = ((), (), s32[]{:S(2)}) async-start(), calls=%async_computation.24 | async-start | bytes 26214400 | tf_op jit(solution)/shard_map/reduce_scatter | solution.py:236
  2063.2 1908.4 %all-reduce.11.cloned.1.call-start = ((), (), s32[]{:S(2)}) async-start(), calls=%async_computation.27 | async-start | bytes 48234496 | tf_op jit(solution)/shard_map/psum | solution.py:316
  3666.6 18.6 slice-start.6
  3666.6 21.5 slice-start.4
  3688.2 36.9 copy-start.40
  (70 other events, 244.3 us)
Sparse Core Ops, SparseCore 0:
  9.6 152.3 all-gather.11
  163.5 147.8 all-gather.17
  313.0 148.0 all-gather.15
  463.0 44.0 all-gather.13
  509.2 44.6 all-gather.19
  555.3 148.3 all-gather.21
  705.2 355.0 all-gather.23
  1061.9 355.3 all-gather.25
  1418.9 355.3 all-gather.27
  1932.7 42.4 reduce-scatter.27
  1978.1 43.1 reduce-scatter.29
  2024.2 143.7 reduce-scatter.13
  2170.3 145.1 reduce-scatter.19
  2318.4 145.1 reduce-scatter.15
  2466.4 145.1 reduce-scatter.17
  2613.8 347.9 reduce-scatter.21
  2964.1 348.6 reduce-scatter.23
  3315.0 348.6 reduce-scatter.25
  3669.7 301.8 all-reduce.10
where the time goes:
time: 4020 us; the launch traced here: 4010 us
  waiting for transfers between devices  3530 us (88%)
  matrix products  211 us (5%)
  local copies, waits for them, and re-layouts  118 us (3%)
  blocking collectives  74.6 us (2%)
  other arithmetic  50.8 us (1%)
    all_gather x1, waiting for transfers between devices, local(): lax.all_gather(w_gate, 'group', axis=1, tiled=True)  352 us
    reduce_scatter x1, waiting for transfers between devices, local(): lax.psum_scatter(inner_rows(normed_two, grad_up).astype(jnp.bfloat16), 'g...  351 us
    reduce_scatter x1, waiting for transfers between devices, local(): lax.psum_scatter(inner_rows(hidden_low, grad_low).astype(jnp.bfloat16), '...  351 us
    reduce_scatter x1, waiting for transfers between devices, local(): lax.psum_scatter(inner_rows(normed_two, grad_gate).astype(jnp.bfloat16),...  350 us
    all_gather x1, waiting for transfers between devices, local(): lax.all_gather(w_ffn_out, 'group', axis=0, tiled=True)  345 us
    all_gather x1, waiting for transfers between devices, local(): lax.all_gather(w_up, 'group', axis=1, tiled=True)  345 us
    psum x1, waiting for transfers between devices, local(): lax.psum(query_part.astype(jnp.bfloat16), 'replica').astype(jnp.float32)  245 us
    reduce_scatter x1, waiting for transfers between devices, local(): lax.psum_scatter(key_grad.astype(jnp.bfloat16), 'group', scatter_dimensio...  148 us
  transfers between devices with their start and end apart: 19, of which 19 were waited for; matrix products, arithmetic and copies ran while one was open for 4% of the time, Pallas kernels for 0%

commit v1 on v0

--- a/solution.py
+++ b/solution.py
@@ -7,6 +7,29 @@
 negative = -1000000000.0
 head_block = 8
 highest = lax.Precision.HIGHEST
+
+
+def mark_the_limits(target, in_dim):
+    carry_in = list(target.shape[1:])
+    carry_in[in_dim] *= target.shape[0]
+    low = jnp.moveaxis(target, 0, in_dim).reshape(carry_in)
+    return low
+
+
+def raise_joints(sheet, peer_axis):
+    kept_arr = lax.axis_size(peer_axis)
+    earlier, near = (kept_arr, lax.axis_index(peer_axis))
+    current_arr, z1 = (sheet[None], 1)
+    while z1 < earlier:
+        a_next = lax.ppermute(
+            current_arr, peer_axis, list(map(lambda at: (at, at ^ z1), range(earlier)))
+        )
+        reached = near & z1 == 0
+        long_array = jnp.where(reached, current_arr, a_next)
+        fresh = jnp.where(reached, a_next, current_arr)
+        current_arr = jnp.concatenate([long_array, fresh])
+        z1 *= 2
+    return current_arr
 
 
 def rms_scale(values, gain):
@@ -154,6 +177,11 @@
     w_ffn_out,
     cotangent,
 ):
+
+    def load_pairs_all(t0, field_in, dim_no):
+        heard = mark_the_limits(raise_joints(t0, field_in), dim_no)
+        return heard
+
     hidden_in = inputs[0].astype(jnp.float32)
     row_count = hidden_in.shape[0]
     keys_total = row_count * lax.axis_size("group")
@@ -168,7 +196,7 @@
         lax.all_gather(w_query, "group", axis=1, tiled=True),
         lax.all_gather(w_key, "group", axis=1, tiled=True),
         lax.all_gather(w_value, "group", axis=1, tiled=True),
-        lax.all_gather(w_attn_out, "group", axis=0, tiled=True),
+        load_pairs_all(w_attn_out, "group", 0),
         lax.all_gather(bias_table, "group", axis=1, tiled=True),
     )
     gain_first = gain_one.astype(jnp.float32)

time: 4020 us -> 4150 us (1.032)
  blocking collectives: 74.6 us -> 376 us
  waiting for transfers between devices: 3530 us -> 3340 us
    all_gather x1, blocking collectives: 15.4 us -> 302 us  [local(): lax.all_gather(norm2_gain, 'group', axis=0, tiled=True)]
    all_gather x1, waiting for transfers between devices: 352 us -> 183 us  [local(): lax.all_gather(w_gate, 'group', axis=1, tiled=True)]
    ppermute x0 -> x2, waiting for transfers between devices: none -> 160 us  [raise_joints(): lax.ppermute(current_arr, peer_axis, list(map(lambda at: (at, at ^ z1), r...]
    all_gather x1, waiting for transfers between devices: 111 us -> 0.01 us  [local(): lax.all_gather(w_query, 'group', axis=1, tiled=True)]
    all_gather x1, waiting for transfers between devices: 42.8 us -> 0.01 us  [local(): lax.all_gather(key_low, 'group', axis=0, tiled=True)]
  transfers between devices with their start and end apart: 19 -> 21, of which waited for: 19 -> 17; matrix products, arithmetic and copies ran while one was open for 4% -> 6% of each run, Pallas kernels for 0% -> 0%
where the time goes in v1:
time: 4150 us; the launch traced here: 4140 us
  waiting for transfers between devices  3340 us (80%)
  blocking collectives  376 us (9%)
  matrix products  213 us (5%)
  local copies, waits for them, and re-layouts  118 us (3%)
  other arithmetic  67.7 us (2%)
    reduce_scatter x1, waiting for transfers between devices, local(): lax.psum_scatter(inner_rows(normed_two, grad_up).astype(jnp.bfloat16), 'g...  351 us
    reduce_scatter x1, waiting for transfers between devices, local(): lax.psum_scatter(inner_rows(hidden_low, grad_low).astype(jnp.bfloat16), '...  351 us
    reduce_scatter x1, waiting for transfers between devices, local(): lax.psum_scatter(inner_rows(normed_two, grad_gate).astype(jnp.bfloat16),...  350 us
    all_gather x1, waiting for transfers between devices, local(): lax.all_gather(w_ffn_out, 'group', axis=0, tiled=True)  345 us
    all_gather x1, waiting for transfers between devices, local(): lax.all_gather(w_up, 'group', axis=1, tiled=True)  345 us
    all_gather x1, blocking collectives, local(): lax.all_gather(norm2_gain, 'group', axis=0, tiled=True)  302 us
    psum x1, waiting for transfers between devices, local(): lax.psum(query_part.astype(jnp.bfloat16), 'replica').astype(jnp.float32)  245 us
    all_gather x1, waiting for transfers between devices, local(): lax.all_gather(w_gate, 'group', axis=1, tiled=True)  183 us
  transfers between devices with their start and end apart: 21, of which 17 were waited for; matrix products, arithmetic and copies ran while one was open for 6% of the time, Pallas kernels for 0%

profile of v1, /device:TPU:0, one launch (start us, length us, event | category | flops | bytes accessed | tf_op | source)
XLA Modules:
  0.0 4135.8 jit_solution(6860282864198943273)
XLA Ops:
  9.5 13.5 all-gather
  23.3 138.7 %all-gather.12.cloned.1.call-done = bf16[2048,2048]{1,0:T(8,128)(2,1)} async-done(((bf16[2048,512]{1,0:T(8,128)(2,1)}), bf16[2048,2048]{1,0:T(8,128)(2,1)}) %all-gather.12.cloned.1.call-update) | async-done | bytes 8388624 | tf_op jit(solution)/shard_map/all_gather | solution.py:198
  167.5 143.9 %all-gather.18.cloned.1.call-done = bf16[2048,2048]{1,0:T(8,128)(2,1)} async-done(((bf16[2048,512]{1,0:T(8,128)(2,1)}), bf16[2048,2048]{1,0:T(8,128)(2,1)}) %all-gather.18.cloned.1.call-update) | async-done | bytes 8388624 | tf_op jit(solution)/shard_map/all_gather | solution.py:197
  320.1 160.0 %collective-permute-done = bf16[1,512,2048]{2,1,0:T(8,128)(2,1)} collective-permute-done((bf16[1,512,2048]{2,1,0:T(8,128)(2,1)S(1)}, bf16[1,512,2048]{2,1,0:T(8,128)(2,1)}, u32[]{:S(2)}, u32[]{:S(2)}) %collective-permute-start) | collective-permute-done | bytes 2097184 | tf_op jit(solution)/shard_map/ppermute | solution.py:24
  485.6 301.5 %all-gather.1 = bf16[4,1,512]{2,1,0:T(2,128)(2,1)S(1)} all-gather(bf16[1,1,512]{2,1,0:T(2,128)(2,1)S(1)} %reshape.203), channel_id=1, replica_groups=mesh['replica'=8,'group'=4] {'group'}, dimensions={0}, use_global_device_ids=true | all-gather | bytes 5120 | tf_op jit(solution)/shard_map/all_gather | solution.py:195
  787.8 29.2 all_gather.49
  845.1 45.2 %while.32 = (s32[]{:T(128)}, bf16[4,128,8,64]{1,3,2,0:T(8,128)(2,1)}, f32[4,8,128]{2,1,0:T(8,128)S(1)}, bf16[4,512,8,64]{1,3,2,0:T(8,128)(2,1)}, bf16[4,128,8,64...) while((s32[]{:T(128)}, ...), condition=%wide.region_4.5_spmd.clone, body=%wide.region_1.4_spmd.clone.sunk | while | flops 138411520 | bytes 35106080 | solution.py:113
  895.5 183.0 %all-gather.22.cloned.1.call-done = bf16[2048,5120]{1,0:T(8,128)(2,1)} async-done(((bf16[2048,1280]{1,0:T(8,128)(2,1)}), bf16[2048,5120]{1,0:T(8,128)(2,1)}) %all-gather.22.cloned.1.call-update) | async-done | bytes 20971536 | tf_op jit(solution)/shard_map/all_gather | solution.py:231
  1078.6 11.8 fusion.89
  1090.4 344.9 %all-gather.24.cloned.1.call-done = bf16[2048,5120]{1,0:T(8,128)(2,1)} async-done(((bf16[2048,1280]{1,0:T(8,128)(2,1)}), bf16[2048,5120]{1,0:T(8,128)(2,1)}) %all-gather.24.cloned.1.call-update) | async-done | bytes 20971536 | tf_op jit(solution)/shard_map/all_gather | solution.py:232
  1435.3 11.7 fusion.90
  1447.0 345.3 %all-gather.26.cloned.1.call-done = bf16[5120,2048]{1,0:T(8,128)(2,1)} async-done(((bf16[1280,2048]{1,0:T(8,128)(2,1)}), bf16[5120,2048]{1,0:T(8,128)(2,1)}) %all-gather.26.cloned.1.call-update) | async-done | bytes 20971536 | tf_op jit(solution)/shard_map/all_gather | solution.py:233
  1792.3 14.6 multiply_convert_fusion.1
  1806.9 12.0 fusion.91
  1819.0 12.2 multiply_reduce_fusion.1
  1831.6 110.6 %all-gather.28.cloned.1.call-done = bf16[2048,2048]{1,0:T(8,128)(2,1)} async-done(((bf16[512,2048]{1,0:T(8,128)(2,1)}), bf16[2048,2048]{1,0:T(8,128)(2,1)}) %all-gather.28.cloned.1.call-update) | async-done | bytes 8388624 | tf_op jit(solution)/shard_map/all_gather | solution.py:279
  1950.4 106.6 %while.33 = (s32[]{:T(128)}, bf16[4,128,8,64]{1,3,2,0:T(8,128)(2,1)}, bf16[4,512,8,64]{1,3,2,0:T(8,128)(2,1)}, bf16[4,512,8,64]{1,3,2,0:T(8,128)(2,1)}, f32[4,8,...) while((s32[]{:T(128)}, ...), condition=%wide.region_10.11_spmd.clone, body=%wide.region_7.10_spmd.clone.sunk | while | flops 341570048 | bytes 102152648 | solution.py:155
  2077.6 25.8 reduce-scatter.28.cloned.1.call-done
  2110.3 39.2 reduce-scatter.30.cloned.1.call-done
  2158.2 10.2 convolution_convert_fusion.2
  2169.7 10.2 convolution_convert_fusion.1
  2191.6 104.5 %reduce-scatter.14.cloned.1.call-done = bf16[2048,512]{1,0:T(8,128)(2,1)} async-done(((bf16[2048,2048]{1,0:T(8,128)(2,1)}), bf16[2048,512]{1,0:T(8,128)(2,1)}) %reduce-scatter.14.cloned.1.call-update) | async-done | bytes 2097168 | tf_op jit(solution)/shard_map/reduce_scatter | solution.py:326
  2296.1 147.6 %reduce-scatter.20.cloned.1.call-done = bf16[512,2048]{1,0:T(8,128)(2,1)} async-done(((bf16[2048,2048]{1,0:T(8,128)(2,1)}), bf16[512,2048]{1,0:T(8,128)(2,1)}) %reduce-scatter.20.cloned.1.call-update) | async-done | bytes 2097168 | tf_op jit(solution)/shard_map/reduce_scatter | solution.py:335
  2443.7 148.0 %reduce-scatter.16.cloned.1.call-done = bf16[2048,512]{1,0:T(8,128)(2,1)} async-done(((bf16[2048,2048]{1,0:T(8,128)(2,1)}), bf16[2048,512]{1,0:T(8,128)(2,1)}) %reduce-scatter.16.cloned.1.call-update) | async-done | bytes 2097168 | tf_op jit(solution)/shard_map/reduce_scatter | solution.py:329
  2591.7 148.0 %reduce-scatter.18.cloned.1.call-done = bf16[2048,512]{1,0:T(8,128)(2,1)} async-done(((bf16[2048,2048]{1,0:T(8,128)(2,1)}), bf16[2048,512]{1,0:T(8,128)(2,1)}) %reduce-scatter.18.cloned.1.call-update) | async-done | bytes 2097168 | tf_op jit(solution)/shard_map/reduce_scatter | solution.py:332
  2739.8 350.2 %reduce-scatter.22.cloned.1.call-done = bf16[2048,1280]{1,0:T(8,128)(2,1)} async-done(((bf16[2048,5120]{1,0:T(8,128)(2,1)}), bf16[2048,1280]{1,0:T(8,128)(2,1)}) %reduce-scatter.22.cloned.1.call-update) | async-done | bytes 5242896 | tf_op jit(solution)/shard_map/reduce_scatter | solution.py:252
  3089.9 351.0 %reduce-scatter.24.cloned.1.call-done = bf16[2048,1280]{1,0:T(8,128)(2,1)} async-done(((bf16[2048,5120]{1,0:T(8,128)(2,1)}), bf16[2048,1280]{1,0:T(8,128)(2,1)}) %reduce-scatter.24.cloned.1.call-update) | async-done | bytes 5242896 | tf_op jit(solution)/shard_map/reduce_scatter | solution.py:258
  3440.9 350.9 %reduce-scatter.26.cloned.1.call-done = bf16[1280,2048]{1,0:T(8,128)(2,1)} async-done(((bf16[5120,2048]{1,0:T(8,128)(2,1)}), bf16[1280,2048]{1,0:T(8,128)(2,1)}) %reduce-scatter.26.cloned.1.call-update) | async-done | bytes 5242896 | tf_op jit(solution)/shard_map/reduce_scatter | solution.py:264
  3801.4 11.9 fusion.51
  3819.4 18.9 all-reduce.8
  3838.5 13.1 all-reduce.6
  3854.5 245.3 %all-reduce.11.cloned.1.call-done = (bf16[2048,512]{1,0:T(8,128)(2,1)}, bf16[2048,512]{1,0:T(8,128)(2,1)}, bf16[2048,512]{1,0:T(8,128)(2,1)}, bf16[512,2048]{1,0...) async-done(((bf16[2048,512]{1,0:T(8,128)(2,1)}, bf16[2048,512]{1,0:T(8,128)(2,1)}, bf16[2048,512]{1,0:T(8,128)(2,1)}, ...) | async-done | bytes 24117264 | tf_op jit(solution)/shard_map/psum | solution.py:344
  (385 shorter events, 309.7 us)
Async XLA Ops:
  7.2 154.8 %all-gather.12.cloned.1.call-start = ((), (), s32[]{:S(2)}) async-start(), calls=%async_computation.9 | async-start | bytes 10485760 | tf_op jit(solution)/shard_map/all_gather | solution.py:198
  7.9 303.5 %all-gather.18.cloned.1.call-start = ((), (), s32[]{:S(2)}) async-start(), calls=%async_computation.12 | async-start | bytes 10485760 | tf_op jit(solution)/shard_map/all_gather | solution.py:197
  8.7 821.9 %all-gather.16.cloned.1.call-start = ((), (), s32[]{:S(2)}) async-start(), calls=%async_computation.11 | async-start | bytes 10485760 | tf_op jit(solution)/shard_map/all_gather | solution.py:196
  9.4 826.9 %all-gather.14.cloned.1.call-start = ((), (), s32[]{:S(2)}) async-start(), calls=%async_computation.10 | async-start | bytes 2621440 | tf_op jit(solution)/shard_map/all_gather | solution.py:216
  23.1 807.5 %copy-start.19 = (f32[4,1,512]{2,1,0:T(1,128)}, f32[4,1,512]{2,1,0:T(1,128)S(1)}, u32[]{:S(2)}) copy-start(f32[4,1,512]{2,1,0:T(1,128)S(1)} %convert_element_type.285) | copy-start | bytes 24580
  23.3 144.2 %copy-start.42 = (f32[128]{0:T(128)}, f32[128]{0:T(128)S(1)}, u32[]{:S(2)}) copy-start(f32[128]{0:T(128)S(1)} %fusion.60) | copy-start | bytes 1540
  23.3 807.3 %copy-start.33 = (f32[128]{0:T(128)}, f32[128]{0:T(128)S(1)}, u32[]{:S(2)}) copy-start(f32[128]{0:T(128)S(1)} %fusion.81) | copy-start | bytes 1540
  167.5 672.7 %all-gather.20.cloned.1.call-start = ((), (), s32[]{:S(2)}) async-start(), calls=%async_computation.13 | async-start | bytes 2621440 | tf_op jit(solution)/shard_map/all_gather | solution.py:215
  316.9 761.7 %all-gather.22.cloned.1.call-start = ((), (), s32[]{:S(2)}) async-start(), calls=%async_computation.14 | async-start | bytes 26214400 | tf_op jit(solution)/shard_map/all_gather | solution.py:231
  317.5 1117.8 %all-gather.24.cloned.1.call-start = ((), (), s32[]{:S(2)}) async-start(), calls=%async_computation.15 | async-start | bytes 26214400 | tf_op jit(solution)/shard_map/all_gather | solution.py:232
  318.2 1474.1 %all-gather.26.cloned.1.call-start = ((), (), s32[]{:S(2)}) async-start(), calls=%async_computation.16 | async-start | bytes 26214400 | tf_op jit(solution)/shard_map/all_gather | solution.py:233
  319.0 1623.2 %all-gather.28.cloned.1.call-start = ((), (), s32[]{:S(2)}) async-start(), calls=%async_computation.17 | async-start | bytes 10485760 | tf_op jit(solution)/shard_map/all_gather | solution.py:279
  320.1 160.0 %collective-permute-start = (bf16[1,512,2048]{2,1,0:T(8,128)(2,1)S(1)}, bf16[1,512,2048]{2,1,0:T(8,128)(2,1)}, u32[]{:S(2)}, u32[]{:S(2)}) collective-permute-start(bf16[1,512,2048]{2,1,0:T(8,128)(2,1)S(1)} %bitcast.279), channel_id=1, source_target_pairs={{0,1},{1,0},{2,3},{3,2},{4,5},{5,4},{6,7},{7,6},{8,9},{9,8},{10,11... | collective-permute-start | bytes 6291464 | tf_op jit(solution)/shard_map/ppermute | solution.py:24
  482.7 305.0 %copy-start.36 = (s32[1023]{0:T(1024)S(1)}, s32[1023]{0:T(1024)}, u32[]{:S(2)}) copy-start(s32[1023]{0:T(1024)} %param.20) | copy-start | bytes 12280
  482.7 305.1 %copy-start.39 = (bf16[32,8]{0,1:T(8,128)(2,1)S(1)}, bf16[32,8]{0,1:T(8,128)(2,1)}, u32[]{:S(2)}) copy-start(bf16[32,8]{0,1:T(8,128)(2,1)} %param.26) | copy-start | bytes 1540
  485.4 332.0 %collective-permute-start.1 = (bf16[2,512,2048]{2,1,0:T(8,128)(2,1)}, bf16[2,512,2048]{2,1,0:T(8,128)(2,1)}, u32[]{:S(2)}, u32[]{:S(2)}) collective-permute-start(bf16[2,512,2048]{2,1,0:T(8,128)(2,1)} %pad_maximum_fusion.1), channel_id=1, source_target_pairs={{0,2},{1,3},{2,0},{3,1},{4,6},{5,7},{6,4},{7,5},{8,10},{9,11},{10,... | collective-permute-start | bytes 12582920 | tf_op jit(solution)/shard_map/ppermute | solution.py:24
  485.4 1617.9 %reduce-scatter.28.cloned.1.call-start = ((), (), s32[]{:S(2)}) async-start(), calls=%async_computation.25 | async-start | bytes 2621440
  787.8 35.2 copy-start.37
  895.3 935.9 %copy-start.3 = (f32[128,2048]{1,0:T(8,128)}, f32[128,2048]{1,0:T(8,128)S(1)}, u32[]{:S(2)}) copy-start(f32[128,2048]{1,0:T(8,128)S(1)} %get-tuple-element.328) | copy-start | bytes 3145732
  895.5 539.8 %copy-start.8 = (bf16[128,2048]{1,0:T(8,128)(2,1)}, bf16[128,2048]{1,0:T(8,128)(2,1)S(1)}, u32[]{:S(2)}) copy-start(bf16[128,2048]{1,0:T(8,128)(2,1)S(1)} %multiply_convert_fusion.3) | copy-start | bytes 1572868
  1090.4 702.0 %copy-start.21 = (bf16[1,128,2048]{2,1,0:T(8,128)(2,1)S(1)}, bf16[1,128,2048]{2,1,0:T(8,128)(2,1)}, u32[]{:S(2)}) copy-start(bf16[1,128,2048]{2,1,0:T(8,128)(2,1)} %param.31) | copy-start | bytes 1572868
  1831.5 116.9 %copy-start.6 = (f32[128,2048]{1,0:T(8,128)}, f32[128,2048]{1,0:T(8,128)S(1)}, u32[]{:S(2)}) copy-start(f32[128,2048]{1,0:T(8,128)S(1)} %fusion.64) | copy-start | bytes 3145732
  2061.1 88.5 %reduce-scatter.30.cloned.1.call-start = ((), (), s32[]{:S(2)}) async-start(), calls=%async_computation.26 | async-start | bytes 2621440
  2063.6 232.6 %reduce-scatter.14.cloned.1.call-start = ((), (), s32[]{:S(2)}) async-start(), calls=%async_computation.18 | async-start | bytes 10485760 | tf_op jit(solution)/shard_map/reduce_scatter | solution.py:326
  2070.6 373.2 %reduce-scatter.20.cloned.1.call-start = ((), (), s32[]{:S(2)}) async-start(), calls=%async_computation.21 | async-start | bytes 10485760 | tf_op jit(solution)/shard_map/reduce_scatter | solution.py:335
  2077.5 514.2 %reduce-scatter.16.cloned.1.call-start = ((), (), s32[]{:S(2)}) async-start(), calls=%async_computation.19 | async-start | bytes 10485760 | tf_op jit(solution)/shard_map/reduce_scatter | solution.py:329
  2110.2 629.5 %reduce-scatter.18.cloned.1.call-start = ((), (), s32[]{:S(2)}) async-start(), calls=%async_computation.20 | async-start | bytes 10485760 | tf_op jit(solution)/shard_map/reduce_scatter | solution.py:332
  2156.4 933.5 %reduce-scatter.22.cloned.1.call-start = ((), (), s32[]{:S(2)}) async-start(), calls=%async_computation.22 | async-start | bytes 26214400 | tf_op jit(solution)/shard_map/reduce_scatter | solution.py:252
  2168.4 1272.5 %reduce-scatter.24.cloned.1.call-start = ((), (), s32[]{:S(2)}) async-start(), calls=%async_computation.23 | async-start | bytes 26214400 | tf_op jit(solution)/shard_map/reduce_scatter | solution.py:258
  2179.9 1612.0 %reduce-scatter.26.cloned.1.call-start = ((), (), s32[]{:S(2)}) async-start(), calls=%async_computation.24 | async-start | bytes 26214400 | tf_op jit(solution)/shard_map/reduce_scatter | solution.py:264
  2191.3 1908.4 %all-reduce.11.cloned.1.call-start = ((), (), s32[]{:S(2)}) async-start(), calls=%async_computation.27 | async-start | bytes 48234496 | tf_op jit(solution)/shard_map/psum | solution.py:344
  3816.3 37.0 copy-start.43
  (73 other events, 285.1 us)
Sparse Core Ops, SparseCore 0:
  9.6 152.3 all-gather.11
  163.5 147.8 all-gather.17
  313.0 202.9 all-gather.15
  518.0 125.3 all-gather.13
  645.3 63.0 all-gather.19
  709.9 368.6 all-gather.21
  1080.1 355.1 all-gather.23
  1436.9 355.3 all-gather.25
  1793.9 148.1 all-gather.27
  2061.2 42.0 reduce-scatter.27
  2106.3 43.1 reduce-scatter.29
  2152.3 143.7 reduce-scatter.13
  2298.5 145.1 reduce-scatter.19
  2446.5 145.1 reduce-scatter.15
  2594.5 145.1 reduce-scatter.17
  2742.0 347.9 reduce-scatter.21
  3092.3 348.6 reduce-scatter.23
  3443.2 348.6 reduce-scatter.25
  3797.8 301.8 all-reduce.10
